TPU v7x, 32 devices: a whole 2x2x4 slice. The times are simulated.
32 devices in a mesh: tiles: 2 (over x), rows: 16 (over z, y, core).
Axes of the slice: x: 2, y: 2, z: 4, core: 2. Of those that a mesh axis runs over, the one named last changes fastest.
Arguments:
- reflect: bfloat16 [128, 6, 32, 2048], P('rows', None, None, 'tiles'), parts along dimension 3, may hold values from 0 to 6.5
- clear_conf: int32 [128, 32, 2048], P('rows', None, 'tiles'), parts along dimension 2, may hold values from 0 to 100
- sun_view: int32 [128, 3, 32, 2048], P('rows', None, None, 'tiles'), parts along dimension 3, may hold values from 0 to 18000, as said below
- sensor_id: int32 [128], replicated, may hold values from 0 to 3
- band_gain: float32 [4, 6], replicated, may hold values from 0.5 to 1.5
- sensor_weight: float32 [4], replicated, may hold values from 0.5 to 2
- prior: float32 [32, 18, 2048], P('rows', None, 'tiles'), parts along dimension 2, may hold values from -1.75 to 1.75
Outputs:
- brdf_weights: float32 [32, 18, 2048], P('rows', None, 'tiles'), parts along dimension 2
There are 2 independent parts, one for each index of `tiles`. A program takes and returns all parts, laid end to end along the dimension named above; an argument that names none is the same for every part. Nothing has to cross between parts.
Inputs may be any that keep to these rules, and one draw needn't show every extreme that they name: `sun_view`: component 0 is the solar zenith, 2000 to 7000; component 1 the view zenith, 0 to 1500; component 2 the relative azimuth, 0 to 18000.
All inputs are finite; a program needn't handle non-finite values.
Results may differ from a plain program's by a relative error of at most 0.0003.
Values may be sent and summed in bfloat16 or wider, within the bound.
A program may use at most 128 MiB of HBM per device.

v0:
```python
import math

import jax
import jax.numpy as jnp
from jax import lax
from jax.sharding import PartitionSpec as P

DATES = 128
ITERS = 3


to_radian = math.pi / 18000.0
prior_pull = 0.1
smooth_pull = 0.5


def with_halo(block, sides, width):
    for axis, dim in sides:
        count = lax.axis_size(axis)
        forward = [(i, i + 1) for i in range(count - 1)]
        backward = [(target, source) for source, target in forward]
        low = lax.ppermute(
            lax.slice_in_dim(block, block.shape[dim] - width, None, axis=dim), axis, forward
        )
        high = lax.ppermute(lax.slice_in_dim(block, 0, width, axis=dim), axis, backward)
        block = jnp.concatenate([low, block, high], axis=dim)
    return block


def ross_li(sun_view):
    solar_zen = sun_view[:, 0].astype(jnp.float32) * to_radian
    view_zen = sun_view[:, 1].astype(jnp.float32) * to_radian
    azimuth = sun_view[:, 2].astype(jnp.float32) * to_radian
    cos_sun, sin_sun = (jnp.cos(solar_zen), jnp.sin(solar_zen))
    cos_view, sin_view = (jnp.cos(view_zen), jnp.sin(view_zen))
    cos_azim, sin_azim = (jnp.cos(azimuth), jnp.sin(azimuth))
    cos_phase = cos_sun * cos_view + sin_sun * sin_view * cos_azim
    phase_angle = jnp.arccos(cos_phase)
    volume = ((0.5 * math.pi - phase_angle) * cos_phase + jnp.sin(phase_angle)) / (
        cos_sun + cos_view
    ) - 0.25 * math.pi
    tan_sun = sin_sun / cos_sun
    tan_view = sin_view / cos_view
    sec_sun = 1.0 / cos_sun
    sec_view = 1.0 / cos_view
    spread = tan_sun * tan_sun + tan_view * tan_view - 2.0 * tan_sun * tan_view * cos_azim
    cross_term = tan_sun * tan_view * sin_azim
    cos_correlation = jnp.minimum(
        2.0 * jnp.sqrt(spread + cross_term * cross_term) / (sec_sun + sec_view), 1.0
    )
    correlation_angle = jnp.arccos(cos_correlation)
    correlation = (
        (correlation_angle - jnp.sin(correlation_angle) * cos_correlation)
        * (sec_sun + sec_view)
        / math.pi
    )
    geometric = correlation - sec_sun - sec_view + 0.5 * (1.0 + cos_phase) * sec_sun * sec_view
    return (volume, geometric)


def normal_terms(reflect, clear_conf, sun_view, date_gain, date_weight):
    volume, geometric = ross_li(sun_view)
    weight = date_weight[:, None, None] * clear_conf.astype(jnp.float32) * 0.01
    weighted_vol = weight * volume
    weighted_geo = weight * geometric
    entries = [
        jnp.sum(weight, 0),
        jnp.sum(weighted_vol, 0),
        jnp.sum(weighted_geo, 0),
        jnp.sum(weighted_vol * volume, 0),
        jnp.sum(weighted_vol * geometric, 0),
        jnp.sum(weighted_geo * geometric, 0),
    ]
    signal = reflect.astype(jnp.float32) * date_gain[:, :, None, None]
    for band_index in range(signal.shape[1]):
        band_signal = signal[:, band_index]
        entries = entries + [
            jnp.sum(weight * band_signal, 0),
            jnp.sum(weighted_vol * band_signal, 0),
            jnp.sum(weighted_geo * band_signal, 0),
        ]
    return jnp.stack(entries, axis=1)


def lookup(date_ids, band_gain, sensor_weight):
    match = (date_ids[:, None] == jnp.arange(band_gain.shape[0], dtype=jnp.int32)[None, :]).astype(
        jnp.float32
    )
    date_gain = jnp.sum(match[:, :, None] * band_gain[None], axis=1)
    date_weight = jnp.sum(match * sensor_weight[None], axis=1)
    return (date_gain, date_weight)


def couple(field, normal):
    row_count, coef_count, col_count = field.shape
    grouped = field.reshape(row_count, coef_count // 3, 3, col_count)
    iso_coef, vol_coef, geo_coef = (grouped[:, :, 0], grouped[:, :, 1], grouped[:, :, 2])
    entry = [normal[:, index_n : index_n + 1] for index_n in range(6)]
    result = jnp.stack(
        [
            entry[0] * iso_coef + entry[1] * vol_coef + entry[2] * geo_coef,
            entry[1] * iso_coef + entry[3] * vol_coef + entry[4] * geo_coef,
            entry[2] * iso_coef + entry[4] * vol_coef + entry[5] * geo_coef,
        ],
        axis=2,
    )
    return result.reshape(row_count, coef_count, col_count)


def apply_system(field, normal, degree):
    padded_rows = with_halo(field, (("rows", 0),), 1)
    padded = jnp.pad(padded_rows, ((0, 0), (0, 0), (1, 1)))
    beside = padded[2:, :, 1:-1] + padded[:-2, :, 1:-1] + padded[1:-1, :, 2:] + padded[1:-1, :, :-2]
    return (
        couple(field, normal)
        + prior_pull * field
        + smooth_pull * (degree[:, None, :] * field - beside)
    )


def paired_sums(vector, image):
    return lax.psum((jnp.sum(vector * vector), jnp.sum(vector * image)), "rows")


def on_device(reflect, clear_conf, sun_view, sensor_id, band_gain, sensor_weight, prior):
    rows_here = prior.shape[0]
    col_count = prior.shape[2]
    dates_here = reflect.shape[0]
    first_date = lax.axis_index("rows") * dates_here
    local_ids = lax.dynamic_slice_in_dim(sensor_id, first_date, dates_here, 0)
    date_gain, date_weight = lookup(local_ids, band_gain, sensor_weight)
    sums = lax.psum_scatter(
        normal_terms(reflect, clear_conf, sun_view, date_gain, date_weight),
        "rows",
        scatter_dimension=0,
        tiled=True,
    )
    sums = sums * (1.0 / DATES)
    normal = sums[:, :6]
    target = sums[:, 6:] + prior_pull * prior
    row_pos = lax.axis_index("rows") * rows_here + jnp.arange(rows_here, dtype=jnp.int32)
    total_rows = rows_here * lax.axis_size("rows")
    col_pos = jnp.arange(col_count, dtype=jnp.int32)
    degree = (
        4.0
        - (row_pos[:, None] == 0).astype(jnp.float32)
        - (row_pos[:, None] == total_rows - 1).astype(jnp.float32)
        - (col_pos[None, :] == 0).astype(jnp.float32)
        - (col_pos[None, :] == col_count - 1).astype(jnp.float32)
    )
    solution = prior
    residual = target - apply_system(prior, normal, degree)
    image = apply_system(residual, normal, degree)
    rho_now, curvature = paired_sums(residual, image)
    alpha = rho_now / curvature
    direction, along = (residual, image)
    for iteration in range(ITERS):
        solution = solution + alpha * direction
        residual = residual - alpha * along
        if iteration + 1 < ITERS:
            image = apply_system(residual, normal, degree)
            rho_next, curvature = paired_sums(residual, image)
            ratio = rho_next / rho_now
            alpha = rho_next / (curvature - ratio * rho_next / alpha)
            direction = residual + ratio * direction
            along = image + ratio * along
            rho_now = rho_next
    return solution


def solution(mesh):
    return jax.shard_map(
        on_device,
        mesh=mesh,
        in_specs=(
            P("rows", None, None, "tiles"),
            P("rows", None, "tiles"),
            P("rows", None, None, "tiles"),
            P(),
            P(),
            P(),
            P("rows", None, "tiles"),
        ),
        out_specs=P("rows", None, "tiles"),
        check_vma=False,
    )
```

profile of v0, /device:TPU:0, one launch (start us, length us, event | category | flops | bytes accessed | tf_op | source)
XLA Modules:
  0.0 247.7 jit_solution(1925297742034288179)
XLA Ops:
  6.5 0.0 reduce-scatter.2.cloned.1.call-start
  6.5 0.7 dynamic_slice.3
  7.3 0.7 select_reduce_fusion
  8.0 0.8 copy.50
  8.8 0.1 multiply_reduce_fusion.26
  8.9 0.0 copy-start
  8.9 0.0 copy-start.2
  8.9 3.0 %convert_multiply_fusion = f32[8,6,32,1024]{3,2,0,1:T(8,128)S(1)} fusion(bf16[8,6,32,1024]{3,2,1,0:T(8,128)(2,1)} %param.7, f32[8,6]{0,1:T(8,128)S(1)} %multiply_reduce_fusion.26), kind=kLoop, calls=%fused_computation | loop fusion | flops 3145728 | bytes 9437376 | tf_op jit(solution)/shard_map/mul | solution.py:74
  11.9 0.0 copy-done
  11.9 0.1 copy-done.2
  12.0 23.8 %fusion.44 = (f32[8,32,1024]{2,1,0:T(8,128)S(1)}, f32[8,32,1024]{2,1,0:T(8,128)S(1)}, f32[8,32,1024]{2,1,0:T(8,128)S(1)}, f32[8,32,1024]{2,1,0:T(8,128)S(1)}) fusion(s32[8,32,1024]{2,1,0:T(8,128)S(1)} %copy-done, f32[8]{0:T(128)S(1)} %select_reduce_fusion, s32[8,3,32,1024]{3,2,1,0:T(8,128)S(1)} %copy-done.2), kind=kLoop, calls=%fused_computation.186 | loop fusion | flops 14680064 | bytes 8388640 | tf_op jit(solution)/shard_map/mul | solution.py:64
  35.9 2.5 %multiply_reduce_fusion = (f32[32,1024]{1,0:T(8,128)S(1)}, f32[32,1024]{1,0:T(8,128)S(1)}, f32[32,1024]{1,0:T(8,128)S(1)}, f32[32,1024]{1,0:T(8,128)S(1)}, f32[3...) fusion(f32[8,32,1024]{2,1,0:T(8,128)S(1)} %get-tuple-element.60, ...), kind=kLoop, calls=%fused_computation.40 | loop fusion | flops 11796480 | bytes 14680096 | tf_op jit(solution)/shard_map/reduce_sum | solution.py:80
  38.9 3.5 %copy.51 = f32[32,24,1024]{2,1,0:T(8,128)} copy(f32[32,24,1024]{2,0,1:T(8,128)S(1)} %bitcast_dynamic-update-slice_fusion) | data formatting | bytes 6291456 | tf_op jit(solution)/shard_map/stack | solution.py:82
  42.4 0.0 copy-start.1
  42.4 0.0 reduce-scatter.2.cloned.1.call-update
  42.4 0.9 copy-done.1
  43.3 0.1 fusion.53
  43.4 1.3 collective-permute-start
  44.7 3.0 %collective-permute-start.1 = (f32[1,18,1024]{2,0,1:T(1,128)S(1)}, f32[1,18,1024]{2,0,1:T(1,128)S(1)}, u32[]{:S(2)}, u32[]{:S(2)}) collective-permute-start(f32[1,18,1024]{2,0,1:T(1,128)S(1)} %get-tuple-element.86), channel_id=1, source_target_pairs={{0,1},{1,2},{2,3},{3,4},{4,5},{5,6},{6,7},{7,8},{8,9},{9,10},{10,1... | collective-permute-start | bytes 221192 | tf_op jit(solution)/shard_map/ppermute | solution.py:22
  47.8 0.1 subtract_subtract_fusion
  47.8 0.0 collective-permute-done
  47.8 0.8 collective-permute-done.1
  48.6 0.6 select_maximum_fusion.6
  49.2 62.3 %reduce-scatter.2.cloned.1.call-done = f32[2,24,1024]{2,1,0:T(8,128)} async-done(((f32[32,24,1024]{2,1,0:T(8,128)}), f32[2,24,1024]{2,1,0:T(8,128)}) %reduce-scatter.2.cloned.1.call-update) | async-done | bytes 196624 | tf_op jit(solution)/shard_map/reduce_scatter | solution.py:132
  111.6 1.1 copy_multiply_fusion
  112.7 0.1 multiply_add_fusion.12
  112.8 0.1 pad_maximum_fusion.8
  112.9 0.6 fusion.35
  113.4 0.1 fusion.52
  113.6 0.1 multiply_add_fusion.9
  113.7 1.3 collective-permute-start.2
  115.0 3.0 %collective-permute-start.3 = (f32[1,18,1024]{2,0,1:T(1,128)S(1)}, f32[1,18,1024]{2,0,1:T(1,128)S(1)}, u32[]{:S(2)}, u32[]{:S(2)}) collective-permute-start(f32[1,18,1024]{2,0,1:T(1,128)S(1)} %get-tuple-element.84), channel_id=1, source_target_pairs={{0,1},{1,2},{2,3},{3,4},{4,5},{5,6},{6,7},{7,8},{8,9},{9,10},{10,1... | collective-permute-start | bytes 221192 | tf_op jit(solution)/shard_map/ppermute | solution.py:22
  118.0 0.1 pad_maximum_fusion.9
  118.1 0.0 collective-permute-done.2
  118.1 0.8 collective-permute-done.3
  118.9 0.6 select_maximum_fusion.4
  119.5 1.3 multiply_reduce_fusion.24
  120.8 32.5 %all-reduce.6 = (f32[]{:T(128)}, f32[]{:T(128)}) all-reduce(f32[]{:T(128)} %get-tuple-element.40, f32[]{:T(128)} %get-tuple-element.39), channel_id=1, replica_groups=mesh['tiles'=2,'rows'=16] {'rows'}, use_global_device_ids=true, to_apply=%region_28.29 | all-reduce | flops 2 | bytes 16 | tf_op jit(solution)/shard_map/psum | solution.py:122
  154.7 0.1 multiply_subtract_fusion.1
  154.8 0.1 fusion.51
  154.9 0.1 multiply_add_fusion.6
  155.0 1.3 collective-permute-start.4
  156.3 3.0 %collective-permute-start.5 = (f32[1,18,1024]{2,0,1:T(1,128)S(1)}, f32[1,18,1024]{2,0,1:T(1,128)S(1)}, u32[]{:S(2)}, u32[]{:S(2)}) collective-permute-start(f32[1,18,1024]{2,0,1:T(1,128)S(1)} %get-tuple-element.82), channel_id=1, source_target_pairs={{0,1},{1,2},{2,3},{3,4},{4,5},{5,6},{6,7},{7,8},{8,9},{9,10},{10,1... | collective-permute-start | bytes 221192 | tf_op jit(solution)/shard_map/ppermute | solution.py:22
  159.4 0.1 pad_maximum_fusion.10
  159.4 0.0 collective-permute-done.4
  159.5 0.8 collective-permute-done.5
  160.3 0.6 select_maximum_fusion.2
  160.9 1.3 multiply_reduce_fusion.22
  162.2 30.6 %all-reduce.5 = (f32[]{:T(128)}, f32[]{:T(128)}) all-reduce(f32[]{:T(128)} %get-tuple-element.38, f32[]{:T(128)} %get-tuple-element.37), channel_id=1, replica_groups=mesh['tiles'=2,'rows'=16] {'rows'}, use_global_device_ids=true, to_apply=%region_32.33 | all-reduce | flops 2 | bytes 16 | tf_op jit(solution)/shard_map/psum | solution.py:122
  197.3 0.1 multiply_subtract_fusion
  197.4 0.1 fusion.50
  197.5 0.1 multiply_add_fusion.3
  197.6 1.3 collective-permute-start.6
  198.9 3.0 %collective-permute-start.7 = (f32[1,18,1024]{2,0,1:T(1,128)S(1)}, f32[1,18,1024]{2,0,1:T(1,128)S(1)}, u32[]{:S(2)}, u32[]{:S(2)}) collective-permute-start(f32[1,18,1024]{2,0,1:T(1,128)S(1)} %get-tuple-element.80), channel_id=1, source_target_pairs={{0,1},{1,2},{2,3},{3,4},{4,5},{5,6},{6,7},{7,8},{8,9},{9,10},{10,1... | collective-permute-start | bytes 221192 | tf_op jit(solution)/shard_map/ppermute | solution.py:22
  202.0 0.1 pad_maximum_fusion.11
  202.0 0.0 collective-permute-done.6
  202.1 0.8 collective-permute-done.7
  202.9 0.6 select_maximum_fusion
  203.5 1.3 fusion.37
  204.8 31.3 %all-reduce.4 = (f32[]{:T(128)}, f32[]{:T(128)}) all-reduce(f32[]{:T(128)} %get-tuple-element.36, f32[]{:T(128)} %get-tuple-element.35), channel_id=1, replica_groups=mesh['tiles'=2,'rows'=16] {'rows'}, use_global_device_ids=true, to_apply=%region_36.37 | all-reduce | flops 2 | bytes 16 | tf_op jit(solution)/shard_map/psum | solution.py:122
  240.0 0.9 multiply_add_fusion
  (28 shorter events, 0.3 us)
Async XLA Ops:
  6.5 105.0 %reduce-scatter.2.cloned.1.call-start = ((), (), s32[]{:S(2)}) async-start(), calls=%async_computation.1 | async-start | bytes 3342336 | tf_op jit(solution)/shard_map/reduce_scatter | solution.py:132
  8.9 3.1 %copy-start = (s32[8,32,1024]{2,1,0:T(8,128)S(1)}, s32[8,32,1024]{2,1,0:T(8,128)}, u32[]{:S(2)}) copy-start(s32[8,32,1024]{2,1,0:T(8,128)} %param.8) | copy-start | bytes 3145732
  8.9 3.2 %copy-start.2 = (s32[8,3,32,1024]{3,2,1,0:T(8,128)S(1)}, s32[8,3,32,1024]{3,2,1,0:T(8,128)}, u32[]{:S(2)}) copy-start(s32[8,3,32,1024]{3,2,1,0:T(8,128)} %param.9) | copy-start | bytes 9437188
  42.4 0.9 copy-start.1
  43.4 4.4 %collective-permute-start = (f32[1,18,1024]{2,0,1:T(1,128)S(1)}, f32[1,18,1024]{2,0,1:T(1,128)S(1)}, u32[]{:S(2)}, u32[]{:S(2)}) collective-permute-start(f32[1,18,1024]{2,0,1:T(1,128)S(1)} %get-tuple-element.87), channel_id=1, source_target_pairs={{1,0},{2,1},{3,2},{4,3},{5,4},{6,5},{7,6},{8,7},{9,8},{10,9},{11,1... | collective-permute-start | bytes 221192 | tf_op jit(solution)/shard_map/ppermute | solution.py:25
  44.7 3.9 %collective-permute-start.1 = (f32[1,18,1024]{2,0,1:T(1,128)S(1)}, f32[1,18,1024]{2,0,1:T(1,128)S(1)}, u32[]{:S(2)}, u32[]{:S(2)}) collective-permute-start(f32[1,18,1024]{2,0,1:T(1,128)S(1)} %get-tuple-element.86), channel_id=1, source_target_pairs={{0,1},{1,2},{2,3},{3,4},{4,5},{5,6},{6,7},{7,8},{8,9},{9,10},{10,1... | collective-permute-start | bytes 221192 | tf_op jit(solution)/shard_map/ppermute | solution.py:22
  113.7 4.4 %collective-permute-start.2 = (f32[1,18,1024]{2,0,1:T(1,128)S(1)}, f32[1,18,1024]{2,0,1:T(1,128)S(1)}, u32[]{:S(2)}, u32[]{:S(2)}) collective-permute-start(f32[1,18,1024]{2,0,1:T(1,128)S(1)} %get-tuple-element.85), channel_id=1, source_target_pairs={{1,0},{2,1},{3,2},{4,3},{5,4},{6,5},{7,6},{8,7},{9,8},{10,9},{11,1... | collective-permute-start | bytes 221192 | tf_op jit(solution)/shard_map/ppermute | solution.py:25
  115.0 3.9 %collective-permute-start.3 = (f32[1,18,1024]{2,0,1:T(1,128)S(1)}, f32[1,18,1024]{2,0,1:T(1,128)S(1)}, u32[]{:S(2)}, u32[]{:S(2)}) collective-permute-start(f32[1,18,1024]{2,0,1:T(1,128)S(1)} %get-tuple-element.84), channel_id=1, source_target_pairs={{0,1},{1,2},{2,3},{3,4},{4,5},{5,6},{6,7},{7,8},{8,9},{9,10},{10,1... | collective-permute-start | bytes 221192 | tf_op jit(solution)/shard_map/ppermute | solution.py:22
  155.0 4.4 %collective-permute-start.4 = (f32[1,18,1024]{2,0,1:T(1,128)S(1)}, f32[1,18,1024]{2,0,1:T(1,128)S(1)}, u32[]{:S(2)}, u32[]{:S(2)}) collective-permute-start(f32[1,18,1024]{2,0,1:T(1,128)S(1)} %get-tuple-element.83), channel_id=1, source_target_pairs={{1,0},{2,1},{3,2},{4,3},{5,4},{6,5},{7,6},{8,7},{9,8},{10,9},{11,1... | collective-permute-start | bytes 221192 | tf_op jit(solution)/shard_map/ppermute | solution.py:25
  156.3 3.9 %collective-permute-start.5 = (f32[1,18,1024]{2,0,1:T(1,128)S(1)}, f32[1,18,1024]{2,0,1:T(1,128)S(1)}, u32[]{:S(2)}, u32[]{:S(2)}) collective-permute-start(f32[1,18,1024]{2,0,1:T(1,128)S(1)} %get-tuple-element.82), channel_id=1, source_target_pairs={{0,1},{1,2},{2,3},{3,4},{4,5},{5,6},{6,7},{7,8},{8,9},{9,10},{10,1... | collective-permute-start | bytes 221192 | tf_op jit(solution)/shard_map/ppermute | solution.py:22
  197.6 4.4 %collective-permute-start.6 = (f32[1,18,1024]{2,0,1:T(1,128)S(1)}, f32[1,18,1024]{2,0,1:T(1,128)S(1)}, u32[]{:S(2)}, u32[]{:S(2)}) collective-permute-start(f32[1,18,1024]{2,0,1:T(1,128)S(1)} %get-tuple-element.81), channel_id=1, source_target_pairs={{1,0},{2,1},{3,2},{4,3},{5,4},{6,5},{7,6},{8,7},{9,8},{10,9},{11,1... | collective-permute-start | bytes 221192 | tf_op jit(solution)/shard_map/ppermute | solution.py:25
  198.9 3.9 %collective-permute-start.7 = (f32[1,18,1024]{2,0,1:T(1,128)S(1)}, f32[1,18,1024]{2,0,1:T(1,128)S(1)}, u32[]{:S(2)}, u32[]{:S(2)}) collective-permute-start(f32[1,18,1024]{2,0,1:T(1,128)S(1)} %get-tuple-element.80), channel_id=1, source_target_pairs={{0,1},{1,2},{2,3},{3,4},{4,5},{5,6},{6,7},{7,8},{8,9},{9,10},{10,1... | collective-permute-start | bytes 221192 | tf_op jit(solution)/shard_map/ppermute | solution.py:22
Sparse Core Ops, SparseCore 0:
  42.5 68.9 reduce-scatter.1
where the time goes:
time: 248 us
  blocking collectives  94.4 us (38%)
  waiting for transfers between devices  65.5 us (26%)
  other arithmetic  40.1 us (16%)
  between operations  23.6 us (10%)
  starting transfers between devices  17.3 us (7%)
  local copies, waits for them, and re-layouts  6.72 us (3%)
    psum x3, blocking collectives, paired_sums(): return lax.psum((jnp.sum(vector * vector), jnp.sum(vector * image)), 'rows')  94.4 us
    reduce_scatter x1, waiting for transfers between devices, on_device(): lax.psum_scatter(normal_terms(reflect, clear_conf, sun_view, date_gain, d...  62.3 us
    mul x1, other arithmetic, normal_terms(): weighted_vol = weight * volume  23.8 us
    ppermute x4, starting transfers between devices, with_halo(): lax.ppermute(lax.slice_in_dim(block, block.shape[dim] - width, None, axis...  12.1 us
    ppermute x4, starting transfers between devices, with_halo(): lax.ppermute(lax.slice_in_dim(block, 0, width, axis=dim), axis, backward)  5.17 us
  transfers between devices with their start and end apart: 9, of which 5 were waited for; matrix products, arithmetic and copies ran while one was open for 0% of the time, Pallas kernels for 0%

commit v1 on v0

v1 whole, which is shorter than its diff:
```python
import math

import jax
import jax.numpy as jnp
from jax import lax
from jax.experimental import pallas as pl
from jax.experimental.pallas import tpu as pltpu
from jax.sharding import PartitionSpec as P

DATES = 128

to_radian = math.pi / 18000.0
prior_pull = 0.1
smooth_pull = 0.5
basis_shift = 3.0

LANES = 128
HALVES = 2
ACOS = (
    1.5707963050,
    -0.2145988016,
    0.0889789874,
    -0.0501743046,
    0.0308918810,
    -0.0170881256,
    0.0066700901,
    -0.0012624911,
)


def root(x):
    return x * lax.rsqrt(jnp.maximum(x, 1e-30))


def arccos_over_root(x):
    total = ACOS[-1]
    for coef in ACOS[-2::-1]:
        total = total * x + coef
    return total


def ross_li(sun, view, azim):
    u = (sun - 4500.0) * to_radian
    u2 = u * u
    sin_u = u * (1.0 + u2 * (-1.0 / 6 + u2 * (1.0 / 120 + u2 * (-1.0 / 5040))))
    cos_u = 1.0 + u2 * (-0.5 + u2 * (1.0 / 24 + u2 * (-1.0 / 720 + u2 * (1.0 / 40320))))
    half = math.sqrt(0.5)
    cos_u = cos_u * half
    sin_u = sin_u * half
    sin_sun = cos_u + sin_u
    cos_sun = cos_u - sin_u
    v = view * to_radian
    v2 = v * v
    sin_view = v * (1.0 + v2 * (-1.0 / 6 + v2 * (1.0 / 120)))
    cos_view = 1.0 + v2 * (-0.5 + v2 * (1.0 / 24 + v2 * (-1.0 / 720)))
    a = (9000.0 - azim) * to_radian
    a2 = a * a
    cos_azim = a * (
        1.0
        + a2
        * (
            -1.0 / 6
            + a2
            * (1.0 / 120 + a2 * (-1.0 / 5040 + a2 * (1.0 / 362880 + a2 * (-1.0 / 39916800))))
        )
    )
    cos_pair = cos_sun * cos_view
    sin_pair = sin_sun * sin_view
    cos_total = cos_sun + cos_view
    inverse = 1.0 / (cos_pair * cos_total)
    inv_pair = inverse * cos_total
    inv_total = inverse * cos_pair
    cos_phase = cos_pair + sin_pair * cos_azim
    phase_root = root(1.0 - cos_phase)
    phase_angle = phase_root * arccos_over_root(cos_phase)
    sin_phase = phase_root * root(1.0 + cos_phase)
    volume = ((0.5 * math.pi - phase_angle) * cos_phase + sin_phase) * inv_total - 0.25 * math.pi
    left = sin_sun * cos_view
    right = sin_view * cos_sun
    spread = (
        left * left
        + right * right
        - 2.0 * left * right * cos_azim
        + sin_pair * sin_pair * (1.0 - cos_azim * cos_azim)
    )
    cos_t = jnp.minimum(2.0 * root(spread) * inv_total, 1.0)
    t_root = root(1.0 - cos_t)
    t_part = t_root * (arccos_over_root(cos_t) - root(1.0 + cos_t) * cos_t)
    geometric = inv_pair * (cos_total * (t_part * (1.0 / math.pi) - 1.0) + 0.5 + 0.5 * cos_phase)
    return volume, geometric


def make_kernel(n, dates, bands, total_rows, cols, rows_here):
    quad = 4
    blocks = n // quad
    tall = quad * rows_here
    width = cols // HALVES
    entries = 6 + 3 * bands
    lines = entries * rows_here
    order = []
    low, high = 0, blocks - 1
    while low <= high:
        order.append(high)
        if low != high:
            order.append(low)
        low, high = low + 1, high - 1
    steps = [(block, half) for block in order for half in range(HALVES)]

    def kernel(
        ids_ref,
        gain_ref,
        sensor_ref,
        prior_ref,
        reflect_hbm,
        conf_hbm,
        angle_hbm,
        out_ref,
        reflect_buf,
        conf_buf,
        angle_buf,
        part,
        core_in,
        pair_in,
        block_in,
        sums,
        field,
        halo,
        moment_out,
        moment_in,
        in_sem,
        core_send,
        core_recv,
        pair_send,
        pair_recv,
        block_send,
        block_recv,
        halo_send,
        halo_recv,
        moment_send,
        moment_recv,
    ):
        me = lax.axis_index("rows")
        core = lax.rem(me, 2)
        pair = lax.rem(me // 2, 2)
        zone = me // quad
        has_low = me > 0
        has_high = me < n - 1

        def loads(block):
            window = pl.ds(block * tall, tall)
            return (
                pltpu.make_async_copy(
                    reflect_hbm.at[:, :, window, :], reflect_buf.at[block], in_sem.at[block, 0]
                ),
                pltpu.make_async_copy(
                    conf_hbm.at[:, window, :], conf_buf.at[block], in_sem.at[block, 1]
                ),
                pltpu.make_async_copy(
                    angle_hbm.at[:, :, window, :], angle_buf.at[block], in_sem.at[block, 2]
                ),
            )

        for block in order:
            for copy in loads(block):
                copy.start()

        def remote(src, dst, send, recv, target):
            return pltpu.make_async_remote_copy(
                src_ref=src,
                dst_ref=dst,
                send_sem=send,
                recv_sem=recv,
                device_id={"rows": target},
                device_id_type=pl.DeviceIdType.MESH,
            )

        zero_halo = jnp.zeros(halo.shape[2:], jnp.float32)

        @pl.when(me == 0)
        def _():
            for level in range(4):
                halo[level, 0] = zero_halo

        @pl.when(me == n - 1)
        def _():
            for level in range(4):
                halo[level, 1] = zero_halo

        barrier = pltpu.get_barrier_semaphore()
        for step in range(1, n):
            pl.semaphore_signal(
                barrier,
                inc=1,
                device_id={"rows": lax.rem(me + step, n)},
                device_id_type=pl.DeviceIdType.MESH,
            )

        for row in range(rows_here):
            for kern in range(3):
                for level in range(4):
                    field[level, row, kern] = jnp.zeros((8, cols), jnp.float32)
                for band in range(bands):
                    line = 3 * band + kern
                    field[0, row, kern, band : band + 1, :] = prior_ref[row, line : line + 1, :]

        scale = 0.01 / DATES

        def compute(step):
            block, half = steps[step]
            if half == 0:
                for copy in loads(block):
                    copy.wait()

            def tile(index, carry):
                start = pl.multiple_of(half * width + index * LANES, LANES)
                place = pl.multiple_of(index * LANES, LANES)
                window = pl.ds(start, LANES)
                total = [None] * entries
                for date in range(dates):
                    sensor = ids_ref[me * dates + date]
                    date_scale = sensor_ref[sensor] * scale
                    sun = angle_buf[block, date, 0, :, window].astype(jnp.float32)
                    view = angle_buf[block, date, 1, :, window].astype(jnp.float32)
                    azim = angle_buf[block, date, 2, :, window].astype(jnp.float32)
                    volume, geometric = ross_li(sun, view, azim)
                    weight = conf_buf[block, date, :, window].astype(jnp.float32) * date_scale
                    weighted_vol = weight * volume
                    weighted_geo = weight * geometric
                    terms = [
                        weight,
                        weighted_vol,
                        weighted_geo,
                        weighted_vol * volume,
                        weighted_vol * geometric,
                        weighted_geo * geometric,
                    ] + [None] * (3 * bands)
                    for band in range(bands):
                        signal = (
                            reflect_buf[block, date, band, :, window].astype(jnp.float32)
                            * gain_ref[sensor, band]
                        )
                        terms[6 + band] = weight * signal
                        terms[6 + bands + band] = weighted_vol * signal
                        terms[6 + 2 * bands + band] = weighted_geo * signal
                    total = [t if s is None else s + t for s, t in zip(total, terms)]
                for entry in range(entries):
                    for owner in range(quad):
                        part[
                            block,
                            half,
                            owner % 2,
                            owner // 2,
                            rows_here * entry : rows_here * entry + rows_here,
                            pl.ds(place, LANES),
                        ] = total[entry][owner * rows_here : (owner + 1) * rows_here]
                return carry

            lax.fori_loop(0, width // LANES, tile, 0)

        def core_copy(step):
            block, half = steps[step]
            return remote(
                part.at[block, half, 1 - core],
                core_in.at[block, half],
                core_send.at[step],
                core_recv.at[step],
                me + 1 - 2 * core,
            )

        def pair_copy(step):
            block, half = steps[step]
            return remote(
                part.at[block, half, core, 1 - pair],
                pair_in.at[block, half],
                pair_send.at[step],
                pair_recv.at[step],
                me + 2 - 4 * pair,
            )

        def block_copy(step, source):
            block, half = steps[step]
            return remote(
                part.at[block, half, core, pair],
                block_in.at[source, half],
                block_send.at[step],
                block_recv.at[source, half],
                block * quad + lax.rem(me, quad),
            )

        def halo_copy(level, up):
            row = 0 if up else rows_here - 1
            side = 1 if up else 0
            return remote(
                field.at[level, row],
                halo.at[level, side],
                halo_send.at[level, side],
                halo_recv.at[level, side],
                me - 1 if up else me + 1,
            )

        def send_halo(level):
            @pl.when(has_low)
            def _():
                halo_copy(level, True).start()

            @pl.when(has_high)
            def _():
                halo_copy(level, False).start()

        def await_halo(level):
            @pl.when(has_low)
            def _():
                halo_copy(level, False).wait_recv()

            @pl.when(has_high)
            def _():
                halo_copy(level, True).wait_recv()

        count = len(steps)
        for step in range(count + 2):
            if step < count:
                compute(step)
                if step == 0:
                    pl.semaphore_wait(barrier, n - 1)
                    send_halo(0)
                core_copy(step).start()
            if 1 <= step <= count:
                last = step - 1
                block, half = steps[last]
                core_copy(last).wait_recv()
                for side in range(2):
                    part[block, half, core, side] = (
                        part[block, half, core, side] + core_in[block, half, side]
                    )
                pair_copy(last).start()
            if step >= 2:
                last = step - 2
                block, half = steps[last]
                pair_copy(last).wait_recv()
                part[block, half, core, pair] = (
                    part[block, half, core, pair] + pair_in[block, half]
                )

                @pl.when(zone != block)
                def _(last=last):
                    block_copy(last, zone).start()

        for half in range(HALVES):
            step = half
            total = part[zone, half, core, pair]
            for shift in range(1, blocks):
                source = lax.rem(zone + shift, blocks)
                block_copy(step, source).wait_recv()
                total = total + block_in[source, half]
            sums[:, half * width : (half + 1) * width] = total

        lane = lax.broadcasted_iota(jnp.int32, (8, cols), 1)
        first_col = lane == 0
        last_col = lane == cols - 1
        edge_cols = first_col.astype(jnp.float32) + last_col.astype(jnp.float32)

        def normal_entry(row, entry):
            line = rows_here * entry + row
            return jnp.broadcast_to(sums[line : line + 1, :], (8, cols))

        pick = ((0, 1, 2), (1, 3, 4), (2, 4, 5))

        def apply(level):
            await_halo(level)
            result = []
            for row in range(rows_here):
                position = me * rows_here + row
                inside = (
                    4.0
                    - (position == 0).astype(jnp.float32)
                    - (position == total_rows - 1).astype(jnp.float32)
                )
                own = prior_pull + smooth_pull * (inside - edge_cols)
                line = []
                for kern in range(3):
                    here = field[level, row, kern]
                    above = halo[level, 0, kern] if row == 0 else field[level, row - 1, kern]
                    below = (
                        halo[level, 1, kern]
                        if row == rows_here - 1
                        else field[level, row + 1, kern]
                    )
                    before = jnp.where(first_col, 0.0, pltpu.roll(here, 1, 1))
                    after = jnp.where(last_col, 0.0, pltpu.roll(here, cols - 1, 1))
                    image = own * here - smooth_pull * (above + below + before + after)
                    for other in range(3):
                        image = image + normal_entry(row, pick[kern][other]) * field[level, row, other]
                    line.append(image)
                result.append(line)
            return result

        cells = [(row, kern) for row in range(rows_here) for kern in range(3)]
        image = apply(0)
        for row, kern in cells:
            for band in range(bands):
                line = rows_here * (6 + bands * kern + band) + row
                field[1, row, kern, band : band + 1, :] = sums[line : line + 1, :]
        for row, kern in cells:
            field[1, row, kern] = (
                field[1, row, kern] + prior_pull * field[0, row, kern] - image[row][kern]
            )
        send_halo(1)

        def inner(left, right):
            total = None
            for row, kern in cells:
                term = left(row, kern) * right(row, kern)
                total = term if total is None else total + term
            return jnp.sum(jnp.sum(total, axis=0, keepdims=True), axis=1, keepdims=True)

        def stored(level):
            return lambda row, kern: field[level, row, kern]

        moments = [inner(stored(1), stored(1))]
        for level in (1, 2):
            image = apply(level)
            for row, kern in cells:
                field[level + 1, row, kern] = image[row][kern] - basis_shift * field[level, row, kern]
            send_halo(level + 1)
            moments.append(inner(stored(level), stored(level + 1)))
            moments.append(inner(stored(level + 1), stored(level + 1)))
        image = apply(3)
        moments.append(
            inner(
                stored(3),
                lambda row, kern: image[row][kern] - basis_shift * field[3, row, kern],
            )
        )
        small_lane = lax.broadcasted_iota(jnp.int32, (1, LANES), 1)
        packed = jnp.zeros((1, LANES), jnp.float32)
        for index, value in enumerate(moments):
            packed = jnp.where(small_lane == index, value, packed)
        moment_out[...] = packed

        def moment_copy(target, source):
            return remote(
                moment_out,
                moment_in.at[source],
                moment_send.at[target],
                moment_recv.at[source],
                target,
            )

        for step in range(1, n):
            moment_copy(lax.rem(me + step, n), me).start()
        gathered = packed
        for step in range(1, n):
            source = lax.rem(me + step, n)
            moment_copy(source, source).wait_recv()
            gathered = gathered + moment_in[source]
        m = [
            jnp.sum(jnp.where(small_lane == index, gathered, 0.0), axis=1, keepdims=True)
            for index in range(len(moments))
        ]

        def form(coefs, with_operator):
            total = 0.0
            for i, a in enumerate(coefs):
                for j, b in enumerate(coefs):
                    moment = m[i + j]
                    if with_operator:
                        moment = m[i + j + 1] + basis_shift * moment
                    total = total + a * b * moment
            return total

        one = jnp.ones((1, 1), jnp.float32)
        residual = [one]
        direction = [one]
        answer = [0.0, 0.0, 0.0]
        rho = m[0]
        for iteration in range(3):
            alpha = rho / form(direction, True)
            answer = [
                a + (alpha * direction[i] if i < len(direction) else 0.0)
                for i, a in enumerate(answer)
            ]
            if iteration < 2:
                image = [basis_shift * d for d in direction] + [0.0]
                for i, d in enumerate(direction):
                    image[i + 1] = image[i + 1] + d
                residual = [
                    (residual[i] if i < len(residual) else 0.0) - alpha * image[i]
                    for i in range(len(image))
                ]
                rho_next = form(residual, False)
                ratio = rho_next / rho
                direction = [
                    residual[i] + (ratio * direction[i] if i < len(direction) else 0.0)
                    for i in range(len(residual))
                ]
                rho = rho_next
        for row, kern in cells:
            value = field[0, row, kern]
            for level in range(3):
                value = value + answer[level] * field[level + 1, row, kern]
            for band in range(bands):
                line = 3 * band + kern
                out_ref[row, line : line + 1, :] = value[band : band + 1]

        for step in range(count):
            core_copy(step).wait_send()
            pair_copy(step).wait_send()

            @pl.when(zone != steps[step][0])
            def _(step=step):
                block_copy(step, zone).wait_send()

        for level in range(4):

            @pl.when(has_low)
            def _(level=level):
                halo_copy(level, True).wait_send()

            @pl.when(has_high)
            def _(level=level):
                halo_copy(level, False).wait_send()

        for step in range(1, n):
            moment_copy(lax.rem(me + step, n), me).wait_send()

    count = len(steps)
    f32 = jnp.float32
    dma = pltpu.SemaphoreType.DMA
    scratch = [
        pltpu.VMEM((blocks, dates, bands, tall, cols), jnp.bfloat16),
        pltpu.VMEM((blocks, dates, tall, cols), jnp.int32),
        pltpu.VMEM((blocks, dates, 3, tall, cols), jnp.int32),
        pltpu.VMEM((blocks, HALVES, 2, 2, lines, width), f32),
        pltpu.VMEM((blocks, HALVES, 2, lines, width), f32),
        pltpu.VMEM((blocks, HALVES, lines, width), f32),
        pltpu.VMEM((blocks, HALVES, lines, width), f32),
        pltpu.VMEM((lines, cols), f32),
        pltpu.VMEM((4, rows_here, 3, 8, cols), f32),
        pltpu.VMEM((4, 2, 3, 8, cols), f32),
        pltpu.VMEM((1, LANES), f32),
        pltpu.VMEM((n, 1, LANES), f32),
        dma((blocks, 3)),
        dma((count,)),
        dma((count,)),
        dma((count,)),
        dma((count,)),
        dma((count,)),
        dma((blocks, HALVES)),
        dma((4, 2)),
        dma((4, 2)),
        dma((n,)),
        dma((n,)),
    ]
    return kernel, scratch


def solution(mesh):
    n = mesh.shape["rows"]

    def on_device(reflect, clear_conf, sun_view, sensor_id, band_gain, sensor_weight, prior):
        dates, bands, total_rows, cols = reflect.shape
        kernel, scratch = make_kernel(n, dates, bands, total_rows, cols, prior.shape[0])
        smem = pl.BlockSpec(memory_space=pltpu.SMEM)
        vmem = pl.BlockSpec(memory_space=pltpu.VMEM)
        hbm = pl.BlockSpec(memory_space=pl.ANY)
        return pl.pallas_call(
            kernel,
            out_shape=jax.ShapeDtypeStruct(prior.shape, jnp.float32),
            in_specs=[smem, smem, smem, vmem, hbm, hbm, hbm],
            out_specs=vmem,
            scratch_shapes=scratch,
            compiler_params=pltpu.CompilerParams(
                collective_id=0, has_side_effects=True, vmem_limit_bytes=60 * 1024 * 1024
            ),
        )(sensor_id, band_gain, sensor_weight, prior, reflect, clear_conf, sun_view)

    return jax.shard_map(
        on_device,
        mesh=mesh,
        in_specs=(
            P("rows", None, None, "tiles"),
            P("rows", None, "tiles"),
            P("rows", None, None, "tiles"),
            P(),
            P(),
            P(),
            P("rows", None, "tiles"),
        ),
        out_specs=P("rows", None, "tiles"),
        check_vma=False,
    )
```

time: 248 us -> 56.5 us (0.23)
  blocking collectives: 94.4 us -> 0 us
  waiting for transfers between devices: 65.5 us -> 0 us
  Pallas kernels: 0 us -> 53 us
  other arithmetic: 40.1 us -> 0 us
  between operations: 23.6 us -> 0.01 us
  starting transfers between devices: 17.3 us -> 0 us
  local copies, waits for them, and re-layouts: 6.72 us -> 3.33 us
    psum x3 -> x0, blocking collectives: 94.4 us -> none  [paired_sums(): return lax.psum((jnp.sum(vector * vector), jnp.sum(vector * image)), 'rows')]
    reduce_scatter x1 -> x0, waiting for transfers between devices: 62.3 us -> none  [on_device(): lax.psum_scatter(normal_terms(reflect, clear_conf, sun_view, date_gain, d...]
    pallas_call x0 -> x1, Pallas kernels: none -> 53 us  [on_device(): pl.pallas_call(kernel, out_shape=jax.ShapeDtypeStruct(prior.shape, jnp.fl...]
    mul x3 -> x0, other arithmetic: 27.9 us -> none  [the longest x1 23.8 us: normal_terms(): weighted_vol = weight * volume]
    ppermute x8 -> x0, starting transfers between devices: 17.3 us -> none  [the longest x4 12.1 us: with_halo(): lax.ppermute(lax.slice_in_dim(block, block.shape[dim] - width, None, axis...]
    reduce_sum x6 -> x0, other arithmetic: 7.2 us -> none  [the longest x3 3.85 us: paired_sums(): return lax.psum((jnp.sum(vector * vector), jnp.sum(vector * image)), 'rows')]
    another operation x2 -> x0, local copies, waits for them, and re-layouts: 3.5 us -> none  [normal_terms(): return jnp.stack(entries, axis=1)]
    ppermute x8 -> x0, waiting for transfers between devices: 3.21 us -> none  [the longest x4 3.2 us: with_halo(): lax.ppermute(lax.slice_in_dim(block, block.shape[dim] - width, None, axis...]
  transfers between devices with their start and end apart: 9 -> 0, of which waited for: 5 -> 0; matrix products, arithmetic and copies ran while one was open for 0% -> 0% of each run, Pallas kernels for 0% -> 0%
where the time goes in v1:
time: 56.5 us; the launch traced here: 56.3 us
  Pallas kernels  53 us (94%)
  local copies, waits for them, and re-layouts  3.33 us (6%)
    pallas_call x1, Pallas kernels, on_device(): pl.pallas_call(kernel, out_shape=jax.ShapeDtypeStruct(prior.shape, jnp.fl...  53 us
    pallas_call x1, local copies, waits for them, and re-layouts, on_device(): pl.pallas_call(kernel, out_shape=jax.ShapeDtypeStruct(prior.shape, jnp.fl...  1.7 us
    unnamed x1, local copies, waits for them, and re-layouts  1.63 us

profile of v1, /device:TPU:0, one launch (start us, length us, event | category | flops | bytes accessed | tf_op | source)
XLA Modules:
  0.0 56.3 jit_solution(2189317306667260645)
XLA Ops:
  0.0 1.6 %copy.8.prior_ref = f32[2,18,1024]{2,1,0:T(8,128)} copy(f32[2,18,1024]{2,0,1:T(2,128)} %param.13) | data formatting | bytes 294912 | tf_op args[6]
  1.6 53.0 %shard_map.73 = f32[2,18,1024]{2,1,0:T(8,128)} custom-call(s32[128]{0:T(128)} %ids_ref.1, f32[4,6]{1,0:T(4,128)} %gain_ref.1, f32[4]{0:T(128)} %sensor_ref.1, f32[2,18,1024]{2,1,0:T(8,128)} %copy.8.prior_ref, bf16[8,6,32,1024]{3,2,1,0:T(8,128)(2,1)} %reflect_hbm.1, s32[8,32,1024]{2,1,0:T(8,128)} %conf_hbm.1, s32[8,3,32,1024]{3,2,1,0:T(8,128)} %angle_hbm.1), custom_call_target="tpu_custom_call" | custom-call | tf_op jit(solution)/shard_map/pallas_call | solution.py:566
  54.6 1.7 %copy.9 = f32[2,18,1024]{2,0,1:T(2,128)} copy(f32[2,18,1024]{2,1,0:T(8,128)} %shard_map.73) | data formatting | bytes 294912 | tf_op jit(solution)/shard_map/pallas_call | solution.py:566

commit v2 on v1

--- a/solution.py
+++ b/solution.py
@@ -13,6 +13,8 @@
 prior_pull = 0.1
 smooth_pull = 0.5
 basis_shift = 3.0
+
+geo_centre = -1.2
 
 LANES = 128
 HALVES = 2
@@ -87,7 +89,7 @@
     t_root = root(1.0 - cos_t)
     t_part = t_root * (arccos_over_root(cos_t) - root(1.0 + cos_t) * cos_t)
     geometric = inv_pair * (cos_total * (t_part * (1.0 / math.pi) - 1.0) + 0.5 + 0.5 * cos_phase)
-    return volume, geometric
+    return volume, geometric - geo_centre
 
 
 def make_kernel(n, dates, bands, total_rows, cols, rows_here):
@@ -97,6 +99,9 @@
     width = cols // HALVES
     entries = 6 + 3 * bands
     lines = entries * rows_here
+    third = lines // 3
+    normal_at = (0, 2 * (2 + bands), 1, 2 * (2 + bands) + 1, 3 + bands, 2 + bands)
+    signal_at = (2, 2 * (2 + bands) + 2, 4 + bands)
     order = []
     low, high = 0, blocks - 1
     while low <= high:
@@ -104,7 +109,7 @@
         if low != high:
             order.append(low)
         low, high = low + 1, high - 1
-    steps = [(block, half) for block in order for half in range(HALVES)]
+    steps = [(block, half) for half in range(HALVES) for block in order]
 
     def kernel(
         ids_ref,
@@ -127,6 +132,14 @@
         halo,
         moment_out,
         moment_in,
+        pair_half_out,
+        pair_half_in,
+        block_half_out,
+        block_half_in,
+        pair_half_send,
+        pair_half_recv,
+        block_half_send,
+        block_half_recv,
         in_sem,
         core_send,
         core_recv,
@@ -201,7 +214,7 @@
                     field[level, row, kern] = jnp.zeros((8, cols), jnp.float32)
                 for band in range(bands):
                     line = 3 * band + kern
-                    field[0, row, kern, band : band + 1, :] = prior_ref[row, line : line + 1, :]
+                    field[0, row, kern, band : band + 1, :] = prior_ref[line, row : row + 1, :]
 
         scale = 0.01 / DATES
 
@@ -226,22 +239,25 @@
                     weight = conf_buf[block, date, :, window].astype(jnp.float32) * date_scale
                     weighted_vol = weight * volume
                     weighted_geo = weight * geometric
-                    terms = [
+                    terms = [None] * entries
+                    products = (
                         weight,
                         weighted_vol,
                         weighted_geo,
                         weighted_vol * volume,
                         weighted_vol * geometric,
                         weighted_geo * geometric,
-                    ] + [None] * (3 * bands)
+                    )
+                    for spot, product in zip(normal_at, products):
+                        terms[spot] = product
                     for band in range(bands):
                         signal = (
                             reflect_buf[block, date, band, :, window].astype(jnp.float32)
                             * gain_ref[sensor, band]
                         )
-                        terms[6 + band] = weight * signal
-                        terms[6 + bands + band] = weighted_vol * signal
-                        terms[6 + 2 * bands + band] = weighted_geo * signal
+                        terms[signal_at[0] + band] = weight * signal
+                        terms[signal_at[1] + band] = weighted_vol * signal
+                        terms[signal_at[2] + band] = weighted_geo * signal
                     total = [t if s is None else s + t for s, t in zip(total, terms)]
                 for entry in range(entries):
                     for owner in range(quad):
@@ -267,24 +283,44 @@
                 me + 1 - 2 * core,
             )
 
-        def pair_copy(step):
+        def pair_copies(step):
             block, half = steps[step]
-            return remote(
-                part.at[block, half, core, 1 - pair],
-                pair_in.at[block, half],
-                pair_send.at[step],
-                pair_recv.at[step],
-                me + 2 - 4 * pair,
-            )
-
-        def block_copy(step, source):
+            target = me + 2 - 4 * pair
+            return (
+                remote(
+                    part.at[block, half, core, 1 - pair, 0:third],
+                    pair_in.at[block, half],
+                    pair_send.at[step],
+                    pair_recv.at[step],
+                    target,
+                ),
+                remote(
+                    pair_half_out.at[block, half],
+                    pair_half_in.at[block, half],
+                    pair_half_send.at[step],
+                    pair_half_recv.at[step],
+                    target,
+                ),
+            )
+
+        def block_copies(step, source):
             block, half = steps[step]
-            return remote(
-                part.at[block, half, core, pair],
-                block_in.at[source, half],
-                block_send.at[step],
-                block_recv.at[source, half],
-                block * quad + lax.rem(me, quad),
+            target = block * quad + lax.rem(me, quad)
+            return (
+                remote(
+                    part.at[block, half, core, pair, 0 : 2 * third],
+                    block_in.at[source, half],
+                    block_send.at[step],
+                    block_recv.at[source, half],
+                    target,
+                ),
+                remote(
+                    block_half_out.at[block, half],
+                    block_half_in.at[source, half],
+                    block_half_send.at[step],
+                    block_half_recv.at[source, half],
+                    target,
+                ),
             )
 
         def halo_copy(level, up):
@@ -328,31 +364,60 @@
                 last = step - 1
                 block, half = steps[last]
                 core_copy(last).wait_recv()
-                for side in range(2):
-                    part[block, half, core, side] = (
-                        part[block, half, core, side] + core_in[block, half, side]
-                    )
-                pair_copy(last).start()
+                other = 1 - pair
+                part[block, half, core, other, 0:third] = (
+                    part[block, half, core, other, 0:third] + core_in[block, half, other, 0:third]
+                )
+                pair_half_out[block, half] = (
+                    part[block, half, core, other, third:lines]
+                    + core_in[block, half, other, third:lines]
+                ).astype(jnp.bfloat16)
+                for copy in pair_copies(last):
+                    copy.start()
+                part[block, half, core, pair] = (
+                    part[block, half, core, pair] + core_in[block, half, pair]
+                )
             if step >= 2:
                 last = step - 2
                 block, half = steps[last]
-                pair_copy(last).wait_recv()
-                part[block, half, core, pair] = (
-                    part[block, half, core, pair] + pair_in[block, half]
+                for copy in pair_copies(last):
+                    copy.wait_recv()
+                part[block, half, core, pair, 0:third] = (
+                    part[block, half, core, pair, 0:third] + pair_in[block, half]
                 )
+                rest = part[block, half, core, pair, third:lines] + pair_half_in[
+                    block, half
+                ].astype(jnp.float32)
+                part[block, half, core, pair, third:lines] = rest
+                block_half_out[block, half] = rest[third:].astype(jnp.bfloat16)
 
                 @pl.when(zone != block)
                 def _(last=last):
-                    block_copy(last, zone).start()
+                    for copy in block_copies(last, zone):
+                        copy.start()
 
         for half in range(HALVES):
-            step = half
-            total = part[zone, half, core, pair]
+            step = steps.index((0, half))
+            total = part[zone, half, core, pair, 0 : 2 * third]
+            small = part[zone, half, core, pair, 2 * third : lines]
             for shift in range(1, blocks):
                 source = lax.rem(zone + shift, blocks)
-                block_copy(step, source).wait_recv()
+                for copy in block_copies(step, source):
+                    copy.wait_recv()
                 total = total + block_in[source, half]
-            sums[:, half * width : (half + 1) * width] = total
+                small = small + block_half_in[source, half].astype(jnp.float32)
+            sums[0 : 2 * third, half * width : (half + 1) * width] = total
+            sums[2 * third : lines, half * width : (half + 1) * width] = small
+
+        def lines_of(spot, length=1):
+            return pl.ds(rows_here * spot, rows_here * length)
+
+        n00, n01, n02, _, n12, n22 = (lines_of(spot) for spot in normal_at)
+        sums[n22] = sums[n22] + 2.0 * geo_centre * sums[n02] + geo_centre**2 * sums[n00]
+        sums[n12] = sums[n12] + geo_centre * sums[n01]
+        sums[n02] = sums[n02] + geo_centre * sums[n00]
+        geo_lines = lines_of(signal_at[2], bands)
+        sums[geo_lines] = sums[geo_lines] + geo_centre * sums[lines_of(signal_at[0], bands)]
 
         lane = lax.broadcasted_iota(jnp.int32, (8, cols), 1)
         first_col = lane == 0
@@ -360,13 +425,12 @@
         edge_cols = first_col.astype(jnp.float32) + last_col.astype(jnp.float32)
 
         def normal_entry(row, entry):
-            line = rows_here * entry + row
+            line = rows_here * normal_at[entry] + row
             return jnp.broadcast_to(sums[line : line + 1, :], (8, cols))
 
         pick = ((0, 1, 2), (1, 3, 4), (2, 4, 5))
 
         def apply(level):
-            await_halo(level)
             result = []
             for row in range(rows_here):
                 position = me * rows_here + row
@@ -379,26 +443,29 @@
                 line = []
                 for kern in range(3):
                     here = field[level, row, kern]
-                    above = halo[level, 0, kern] if row == 0 else field[level, row - 1, kern]
-                    below = (
-                        halo[level, 1, kern]
-                        if row == rows_here - 1
-                        else field[level, row + 1, kern]
-                    )
                     before = jnp.where(first_col, 0.0, pltpu.roll(here, 1, 1))
                     after = jnp.where(last_col, 0.0, pltpu.roll(here, cols - 1, 1))
-                    image = own * here - smooth_pull * (above + below + before + after)
+                    beside = before + after
+                    if row > 0:
+                        beside = beside + field[level, row - 1, kern]
+                    if row < rows_here - 1:
+                        beside = beside + field[level, row + 1, kern]
+                    image = own * here - smooth_pull * beside
                     for other in range(3):
                         image = image + normal_entry(row, pick[kern][other]) * field[level, row, other]
                     line.append(image)
                 result.append(line)
+            await_halo(level)
+            for kern in range(3):
+                result[0][kern] = result[0][kern] - smooth_pull * halo[level, 0, kern]
+                result[-1][kern] = result[-1][kern] - smooth_pull * halo[level, 1, kern]
             return result
 
         cells = [(row, kern) for row in range(rows_here) for kern in range(3)]
         image = apply(0)
         for row, kern in cells:
             for band in range(bands):
-                line = rows_here * (6 + bands * kern + band) + row
+                line = rows_here * (signal_at[kern] + band) + row
                 field[1, row, kern, band : band + 1, :] = sums[line : line + 1, :]
         for row, kern in cells:
             field[1, row, kern] = (
@@ -500,15 +567,17 @@
                 value = value + answer[level] * field[level + 1, row, kern]
             for band in range(bands):
                 line = 3 * band + kern
-                out_ref[row, line : line + 1, :] = value[band : band + 1]
+                out_ref[line, row : row + 1, :] = value[band : band + 1]
 
         for step in range(count):
             core_copy(step).wait_send()
-            pair_copy(step).wait_send()
+            for copy in pair_copies(step):
+                copy.wait_send()
 
             @pl.when(zone != steps[step][0])
             def _(step=step):
-                block_copy(step, zone).wait_send()
+                for copy in block_copies(step, zone):
+                    copy.wait_send()
 
         for level in range(4):
 
@@ -532,13 +601,21 @@
         pltpu.VMEM((blocks, dates, 3, tall, cols), jnp.int32),
         pltpu.VMEM((blocks, HALVES, 2, 2, lines, width), f32),
         pltpu.VMEM((blocks, HALVES, 2, lines, width), f32),
-        pltpu.VMEM((blocks, HALVES, lines, width), f32),
-        pltpu.VMEM((blocks, HALVES, lines, width), f32),
+        pltpu.VMEM((blocks, HALVES, lines // 3, width), f32),
+        pltpu.VMEM((blocks, HALVES, 2 * lines // 3, width), f32),
         pltpu.VMEM((lines, cols), f32),
         pltpu.VMEM((4, rows_here, 3, 8, cols), f32),
         pltpu.VMEM((4, 2, 3, 8, cols), f32),
         pltpu.VMEM((1, LANES), f32),
         pltpu.VMEM((n, 1, LANES), f32),
+        pltpu.VMEM((blocks, HALVES, 2 * lines // 3, width), jnp.bfloat16),
+        pltpu.VMEM((blocks, HALVES, 2 * lines // 3, width), jnp.bfloat16),
+        pltpu.VMEM((blocks, HALVES, lines // 3, width), jnp.bfloat16),
+        pltpu.VMEM((blocks, HALVES, lines // 3, width), jnp.bfloat16),
+        dma((count,)),
+        dma((count,)),
+        dma((count,)),
+        dma((blocks, HALVES)),
         dma((blocks, 3)),
         dma((count,)),
         dma((count,)),
@@ -563,16 +640,18 @@
         smem = pl.BlockSpec(memory_space=pltpu.SMEM)
         vmem = pl.BlockSpec(memory_space=pltpu.VMEM)
         hbm = pl.BlockSpec(memory_space=pl.ANY)
-        return pl.pallas_call(
+        stored = prior.transpose(1, 0, 2)
+        solved = pl.pallas_call(
             kernel,
-            out_shape=jax.ShapeDtypeStruct(prior.shape, jnp.float32),
+            out_shape=jax.ShapeDtypeStruct(stored.shape, jnp.float32),
             in_specs=[smem, smem, smem, vmem, hbm, hbm, hbm],
             out_specs=vmem,
             scratch_shapes=scratch,
             compiler_params=pltpu.CompilerParams(
                 collective_id=0, has_side_effects=True, vmem_limit_bytes=60 * 1024 * 1024
             ),
-        )(sensor_id, band_gain, sensor_weight, prior, reflect, clear_conf, sun_view)
+        )(sensor_id, band_gain, sensor_weight, stored, reflect, clear_conf, sun_view)
+        return solved.transpose(1, 0, 2)
 
     return jax.shard_map(
         on_device,

time: 56.5 us -> 51.3 us (0.908)
  Pallas kernels: 53 us -> 49.6 us
  local copies, waits for them, and re-layouts: 3.33 us -> 1.58 us
    pallas_call x1, Pallas kernels: 53 us -> 49.6 us  [on_device(): pl.pallas_call(kernel, out_shape=jax.ShapeDtypeStruct(stored.shape, jnp.f...]
    pallas_call x1 -> x0, local copies, waits for them, and re-layouts: 1.7 us -> none  [on_device(): pl.pallas_call(kernel, out_shape=jax.ShapeDtypeStruct(prior.shape, jnp.fl...]
where the time goes in v2:
time: 51.3 us; the launch traced here: 51.2 us
  Pallas kernels  49.6 us (97%)
  local copies, waits for them, and re-layouts  1.58 us (3%)
    pallas_call x1, Pallas kernels, on_device(): pl.pallas_call(kernel, out_shape=jax.ShapeDtypeStruct(stored.shape, jnp.f...  49.6 us
    unnamed x1, local copies, waits for them, and re-layouts  1.58 us

profile of v2, /device:TPU:0, one launch (start us, length us, event | category | flops | bytes accessed | tf_op | source)
XLA Modules:
  0.0 51.2 jit_solution(14574926593600901869)
XLA Ops:
  0.0 49.6 %shard_map.73 = f32[18,2,1024]{2,1,0:T(2,128)} custom-call(s32[128]{0:T(128)} %ids_ref.1, f32[4,6]{1,0:T(4,128)} %gain_ref.1, f32[4]{0:T(128)} %sensor_ref.1, f32[18,2,1024]{2,1,0:T(2,128)} %bitcast.3, bf16[8,6,32,1024]{3,2,1,0:T(8,128)(2,1)} %reflect_hbm.1, s32[8,32,1024]{2,1,0:T(8,128)} %conf_hbm.1, s32[8,3,32,1024]{3,2,1,0:T(8,128)} %angle_hbm.1), custom_call_target="tpu_custom_call" | custom-call | tf_op jit(solution)/shard_map/pallas_call | solution.py:644
  49.6 1.6 %copy.9 = f32[2,18,1024]{2,0,1:T(2,128)} copy(f32[2,18,1024]{2,0,1:T(2,128)} %bitcast.2) | data formatting | bytes 294912

commit v3 on v2

--- a/solution.py
+++ b/solution.py
@@ -18,6 +18,8 @@
 
 LANES = 128
 HALVES = 2
+CORE_LAG = 2
+PAIR_LAG = 5
 ACOS = (
     1.5707963050,
     -0.2145988016,
@@ -353,15 +355,15 @@
                 halo_copy(level, True).wait_recv()
 
         count = len(steps)
-        for step in range(count + 2):
+        for step in range(count + PAIR_LAG):
             if step < count:
                 compute(step)
                 if step == 0:
                     pl.semaphore_wait(barrier, n - 1)
                     send_halo(0)
                 core_copy(step).start()
-            if 1 <= step <= count:
-                last = step - 1
+            if CORE_LAG <= step < count + CORE_LAG:
+                last = step - CORE_LAG
                 block, half = steps[last]
                 core_copy(last).wait_recv()
                 other = 1 - pair
@@ -377,8 +379,8 @@
                 part[block, half, core, pair] = (
                     part[block, half, core, pair] + core_in[block, half, pair]
                 )
-            if step >= 2:
-                last = step - 2
+            if step >= PAIR_LAG:
+                last = step - PAIR_LAG
                 block, half = steps[last]
                 for copy in pair_copies(last):
                     copy.wait_recv()

time: 51.3 us -> 47.7 us (0.930)
  Pallas kernels: 49.6 us -> 46 us
    pallas_call x1, Pallas kernels: 49.6 us -> 46 us  [on_device(): pl.pallas_call(kernel, out_shape=jax.ShapeDtypeStruct(stored.shape, jnp.f...]
where the time goes in v3:
time: 47.7 us; the launch traced here: 47.6 us
  Pallas kernels  46 us (96%)
  local copies, waits for them, and re-layouts  1.58 us (3%)
    pallas_call x1, Pallas kernels, on_device(): pl.pallas_call(kernel, out_shape=jax.ShapeDtypeStruct(stored.shape, jnp.f...  46 us
    unnamed x1, local copies, waits for them, and re-layouts  1.58 us

profile of v3, /device:TPU:0, one launch (start us, length us, event | category | flops | bytes accessed | tf_op | source)
XLA Modules:
  0.0 47.6 jit_solution(1146968457463023820)
XLA Ops:
  0.0 46.0 %shard_map.73 = f32[18,2,1024]{2,1,0:T(2,128)} custom-call(s32[128]{0:T(128)} %ids_ref.1, f32[4,6]{1,0:T(4,128)} %gain_ref.1, f32[4]{0:T(128)} %sensor_ref.1, f32[18,2,1024]{2,1,0:T(2,128)} %bitcast.3, bf16[8,6,32,1024]{3,2,1,0:T(8,128)(2,1)} %reflect_hbm.1, s32[8,32,1024]{2,1,0:T(8,128)} %conf_hbm.1, s32[8,3,32,1024]{3,2,1,0:T(8,128)} %angle_hbm.1), custom_call_target="tpu_custom_call" | custom-call | tf_op jit(solution)/shard_map/pallas_call | solution.py:646
  46.0 1.6 %copy.9 = f32[2,18,1024]{2,0,1:T(2,128)} copy(f32[2,18,1024]{2,0,1:T(2,128)} %bitcast.2) | data formatting | bytes 294912
